TPU v7x, 32 devices: a whole 2x2x4 slice. The times are simulated.
32 devices in a mesh: shot: 8 (over y, x, core), pair: 4 (over z).
Axes of the slice: x: 2, y: 2, z: 4, core: 2. Of those that a mesh axis runs over, the one named last changes fastest.
Arguments:
- spectra: bfloat16 [2, 128, 128, 1024], P(None, 'shot', None, 'pair'), may hold values from -6 to 6
- shot_weight: float32 [128], P('shot'), may hold values from 0.5 to 2
Outputs:
- virtual_gather: bfloat16 [2, 128, 1024, 1024], P(None, 'shot', 'pair')
All inputs are finite; a program needn't handle non-finite values.
Results may differ from a plain program's by a relative error of at most 0.0054.
Values may be sent and summed in bfloat16 or wider, within the bound.
A program may use at most 128 MiB of HBM per device.

v0:
```python
import jax
import jax.numpy as jnp
from jax import lax
from jax.sharding import PartitionSpec as P


def gram_block(row_data, column_data, factor):
    swapped = jnp.stack([-row_data[1], row_data[0]])
    left_side = jnp.stack([row_data, swapped])
    product = jnp.einsum(
        "ocsfa,csfb->ofab", left_side, column_data, preferred_element_type=jnp.float32
    )
    return product * factor


def shards(spectra, shot_weight):
    scaled = (spectra.astype(jnp.float32) * shot_weight[None, :, None, None]).astype(jnp.bfloat16)
    by_freq = lax.all_to_all(scaled, "shot", split_axis=2, concat_axis=1, tiled=True)
    total_shots = by_freq.shape[1]
    factor = total_shots ** (-0.5)
    full_rows = gram_block(by_freq, lax.all_gather(by_freq, "pair", axis=3, tiled=True), factor)
    return full_rows.astype(jnp.bfloat16)


def solution(mesh):
    return jax.shard_map(
        shards,
        mesh=mesh,
        in_specs=(P(None, "shot", None, "pair"), P("shot")),
        out_specs=P(None, "shot", "pair", None),
        check_vma=False,
    )
```

profile of v0, /device:TPU:0, one launch (start us, length us, event | category | flops | bytes accessed | tf_op | source)
XLA Modules:
  0.0 237.3 jit_solution(6709182819881926623)
XLA Ops:
  6.5 0.0 all-gather.2.cloned.1.call-start
  6.5 2.8 %multiply_convert_fusion = bf16[2,16,128,256]{3,1,0,2:T(8,128)(2,1)S(1)} fusion(bf16[2,16,128,256]{3,2,1,0:T(8,128)(2,1)} %param.2, f32[16]{0:T(128)} %param.3), kind=kLoop, calls=%fused_computation.7 | loop fusion | flops 3145728 | bytes 4194368 | tf_op jit(solution)/shard_map/convert_element_type | solution.py:17
  9.4 31.6 %all_to_all.18 = bf16[2,16,128,256]{3,1,0,2:T(8,128)(2,1)S(1)} all-to-all(bf16[2,16,128,256]{3,1,0,2:T(8,128)(2,1)S(1)} %multiply_convert_fusion), channel_id=1, replica_groups=mesh['shot'=8,'pair'=4] {'shot'}, dimensions={2} | all-to-all | bytes 4194304 | tf_op jit(solution)/shard_map/all_to_all | solution.py:18
  40.9 2.5 %copy.20 = bf16[2,8,16,16,256]{4,3,2,1,0:T(8,128)(2,1)} copy(bf16[2,8,16,16,256]{4,2,0,3,1:T(8,128)(2,1)S(1)} %bitcast.25) | data formatting | bytes 4194304 | tf_op jit(solution)/shard_map/all_to_all | solution.py:18
  43.4 4.6 %copy.21 = bf16[2,128,16,256]{1,3,0,2:T(8,128)(2,1)} copy(bf16[2,128,16,256]{3,2,1,0:T(8,128)(2,1)} %bitcast.28) | data formatting | bytes 4194304 | tf_op jit(solution)/shard_map/all_to_all | solution.py:18
  48.0 0.0 all-gather.2.cloned.1.call-update
  48.0 1.6 copy.22
  49.6 1.2 copy.19
  50.8 0.1 slice_negate_fusion
  50.9 0.0 copy-start
  50.9 0.6 copy.23
  51.5 0.6 copy.24
  52.1 1.5 maximum_bitcast_fusion
  53.6 143.5 %all-gather.2.cloned.1.call-done = bf16[2,128,16,1024]{1,3,0,2:T(8,128)(2,1)} async-done(((bf16[2,128,16,256]{1,3,0,2:T(8,128)(2,1)}), bf16[2,128,16,1024]{1,3,0,2:T(8,128)(2,1)}) %all-gather.2.cloned.1.call-update) | async-done | bytes 8388624 | tf_op jit(solution)/shard_map/all_gather | solution.py:21
  197.2 0.0 copy-done
  197.2 11.0 %fusion.1 = bf16[2,16,256,1024]{2,3,0,1:T(8,128)(2,1)} fusion(bf16[2,128,16,1024]{1,3,0,2:T(8,128)(2,1)} %all-gather.2.cloned.1.call-done, bf16[1,2,128,16,256]{4,2,1,0,3:T(8,128)(2,1)} %maximum_bitcast_fusion, bf16[1,2,128,16,256]{4,2,1,0,3:T(8,128)(2,1)S(1)} %bitcast.31), kind=kOutput, calls=%fused_computation.2 | convolution fusion | flops 4320133120 | bytes 29360128 | tf_op jit(solution)/shard_map/ocsfa,csfb->ofab/dot_general | solution.py:10
  208.1 22.4 %copy.25 = bf16[2,16,256,1024]{3,2,1,0:T(8,128)(2,1)} copy(bf16[2,16,256,1024]{2,3,0,1:T(8,128)(2,1)} %fusion.1) | data formatting | bytes 33554432 | tf_op jit(solution)/shard_map/convert_element_type | solution.py:22
Async XLA Ops:
  6.5 190.6 %all-gather.2.cloned.1.call-start = ((), (), s32[]{:S(2)}) async-start(), calls=%async_computation.1 | async-start | bytes 10485760 | tf_op jit(solution)/shard_map/all_gather | solution.py:21
  50.9 146.2 %copy-start = (bf16[2,8,16,16,256]{4,2,1,0,3:T(8,128)(2,1)S(1)}, bf16[2,8,16,16,256]{4,2,1,0,3:T(8,128)(2,1)}, u32[]{:S(2)}) copy-start(bf16[2,8,16,16,256]{4,2,1,0,3:T(8,128)(2,1)} %copy.22) | copy-start | bytes 6291460
Sparse Core Ops, SparseCore 0:
  48.1 148.9 all-gather.1
where the time goes:
time: 238 us; the launch traced here: 237 us
  waiting for transfers between devices  144 us (61%)
  local copies, waits for them, and re-layouts  33.4 us (14%)
  blocking collectives  31.6 us (13%)
  between operations  13.4 us (6%)
  matrix products  11 us (5%)
  other arithmetic  4.48 us (2%)
    all_gather x1, waiting for transfers between devices, shards(): lax.all_gather(by_freq, 'pair', axis=3, tiled=True)  144 us
    all_to_all x1, blocking collectives, shards(): lax.all_to_all(scaled, 'shot', split_axis=2, concat_axis=1, tiled=True)  31.6 us
    convert_element_type x1, local copies, waits for them, and re-layouts, shards(): return full_rows.astype(jnp.bfloat16)  22.4 us
    dot_general x1, matrix products, gram_block(): jnp.einsum('ocsfa,csfb->ofab', left_side, column_data, preferred_element_...  11 us
    all_to_all x4, local copies, waits for them, and re-layouts, shards(): lax.all_to_all(scaled, 'shot', split_axis=2, concat_axis=1, tiled=True)  9.82 us
  transfers between devices with their start and end apart: 1, of which 1 were waited for; matrix products, arithmetic and copies ran while one was open for 2% of the time, Pallas kernels for 0%

commit v1 on v0

--- a/solution.py
+++ b/solution.py
@@ -18,7 +18,13 @@
     by_freq = lax.all_to_all(scaled, "shot", split_axis=2, concat_axis=1, tiled=True)
     total_shots = by_freq.shape[1]
     factor = total_shots ** (-0.5)
-    full_rows = gram_block(by_freq, lax.all_gather(by_freq, "pair", axis=3, tiled=True), factor)
+    full_rows = gram_block(
+        by_freq,
+        jnp.concatenate(
+            lax.all_to_all(jnp.stack([by_freq] * lax.axis_size("pair")), "pair", 0, 0), axis=3
+        ),
+        factor,
+    )
     return full_rows.astype(jnp.bfloat16)
 
 

time: 238 us -> 277 us (1.16)
  waiting for transfers between devices: 144 us -> 179 us
  between operations: 13.4 us -> 0.04 us
  local copies, waits for them, and re-layouts: 33.4 us -> 44.7 us
  starting transfers between devices: 0.01 us -> 5.63 us
    all_to_all x0 -> x1, waiting for transfers between devices: none -> 179 us  [shards(): lax.all_to_all(jnp.stack([by_freq] * lax.axis_size('pair')), 'pair', 0, 0)]
    all_gather x1 -> x0, waiting for transfers between devices: 144 us -> none  [shards(): lax.all_gather(by_freq, 'pair', axis=3, tiled=True)]
    another operation x0 -> x2, local copies, waits for them, and re-layouts: none -> 9.47 us  [shards(): jnp.stack([by_freq] * lax.axis_size('pair'))]
    reshape x0 -> x1, local copies, waits for them, and re-layouts: none -> 8.04 us  [shards(): jnp.concatenate(lax.all_to_all(jnp.stack([by_freq] * lax.axis_size('pair'...]
    all_to_all x4 -> x2, local copies, waits for them, and re-layouts: 9.82 us -> 3.45 us  [shards(): lax.all_to_all(scaled, 'shot', split_axis=2, concat_axis=1, tiled=True)]
    all_to_all x0 -> x1, starting transfers between devices: none -> 5.63 us  [shards(): lax.all_to_all(jnp.stack([by_freq] * lax.axis_size('pair')), 'pair', 0, 0)]
  transfers between devices with their start and end apart: 1 -> 1, of which waited for: 1 -> 1; matrix products, arithmetic and copies ran while one was open for 2% -> 1% of each run, Pallas kernels for 0% -> 0%
where the time goes in v1:
time: 277 us; the launch traced here: 276 us
  waiting for transfers between devices  179 us (65%)
  local copies, waits for them, and re-layouts  44.7 us (16%)
  blocking collectives  31.6 us (11%)
  matrix products  11.6 us (4%)
  starting transfers between devices  5.63 us (2%)
  other arithmetic  3.17 us (1%)
    all_to_all x1, waiting for transfers between devices, shards(): lax.all_to_all(jnp.stack([by_freq] * lax.axis_size('pair')), 'pair', 0, 0)  179 us
    all_to_all x1, blocking collectives, shards(): lax.all_to_all(scaled, 'shot', split_axis=2, concat_axis=1, tiled=True)  31.6 us
    convert_element_type x1, local copies, waits for them, and re-layouts, shards(): return full_rows.astype(jnp.bfloat16)  22.4 us
    dot_general x1, matrix products, gram_block(): jnp.einsum('ocsfa,csfb->ofab', left_side, column_data, preferred_element_...  11.6 us
    another operation x2, local copies, waits for them, and re-layouts, shards(): jnp.stack([by_freq] * lax.axis_size('pair'))  9.47 us
    reshape x1, local copies, waits for them, and re-layouts, shards(): jnp.concatenate(lax.all_to_all(jnp.stack([by_freq] * lax.axis_size('pair'...  8.04 us
    all_to_all x1, starting transfers between devices, shards(): lax.all_to_all(jnp.stack([by_freq] * lax.axis_size('pair')), 'pair', 0, 0)  5.63 us
  transfers between devices with their start and end apart: 1, of which 1 were waited for; matrix products, arithmetic and copies ran while one was open for 1% of the time, Pallas kernels for 0%

profile of v1, /device:TPU:0, one launch (start us, length us, event | category | flops | bytes accessed | tf_op | source)
XLA Modules:
  0.0 275.9 jit_solution(15598127306906102214)
XLA Ops:
  0.0 2.8 %multiply_convert_fusion = bf16[2,16,128,256]{3,1,0,2:T(8,128)(2,1)S(1)} fusion(bf16[2,16,128,256]{3,2,1,0:T(8,128)(2,1)} %param.2, f32[16]{0:T(128)} %param.3), kind=kLoop, calls=%fused_computation.6 | loop fusion | flops 3145728 | bytes 4194368 | tf_op jit(solution)/shard_map/convert_element_type | solution.py:17
  2.8 31.6 %all_to_all.20 = bf16[2,16,128,256]{3,1,0,2:T(8,128)(2,1)S(1)} all-to-all(bf16[2,16,128,256]{3,1,0,2:T(8,128)(2,1)S(1)} %multiply_convert_fusion), channel_id=1, replica_groups=mesh['shot'=8,'pair'=4] {'shot'}, dimensions={2} | all-to-all | bytes 4194304 | tf_op jit(solution)/shard_map/all_to_all | solution.py:18
  34.4 0.0 copy-start
  34.4 1.3 copy-done
  35.8 0.3 copy.19
  36.0 2.4 copy.9
  38.4 7.1 %stack.23 = bf16[4,2,128,16,256]{2,4,1,3,0:T(8,128)(2,1)} broadcast(bf16[2,128,16,256]{1,3,0,2:T(8,128)(2,1)} %copy.9), dimensions={1,2,3,4} | broadcast | bytes 10485760 | tf_op jit(solution)/shard_map/stack | solution.py:24
  45.5 5.6 %all-to-all-start.1 = ((bf16[4,2,128,16,256]{2,4,1,3,0:T(8,128)(2,1)}), bf16[4,2,128,16,256]{2,4,1,3,0:T(8,128)(2,1)}, u32[]{:S(2)}, u32[]{:S(2)}) async-start(bf16[4,2,128,16,256]{2,4,1,3,0:T(8,128)(2,1)} %stack.23), calls=%async_computation.1 | async-start | bytes 16777216 | tf_op jit(solution)/shard_map/all_to_all | solution.py:24
  51.1 3.2 %copy.11 = bf16[2,8,16,16,256]{4,2,1,0,3:T(8,128)(2,1)} copy(bf16[2,8,16,16,256]{4,2,0,3,1:T(8,128)(2,1)} %bitcast.32) | data formatting | bytes 4194304 | tf_op jit(solution)/shard_map/all_to_all | solution.py:18
  54.3 0.1 slice_negate_fusion
  54.5 0.2 maximum_bitcast_fusion
  54.7 179.3 %all-to-all-done.1 = bf16[4,2,128,16,256]{2,4,1,3,0:T(8,128)(2,1)} async-done(((bf16[4,2,128,16,256]{2,4,1,3,0:T(8,128)(2,1)}), bf16[4,2,128,16,256]{2,4,1,3,0:T(8,128)(2,1)}, u32[]{:S(2)}, u32[]{:S(2)}) %all-to-all-start.1) | async-done | bytes 8388640 | tf_op jit(solution)/shard_map/all_to_all | solution.py:24
  233.9 0.0 copy-start.1
  233.9 8.0 %copy.10 = bf16[2,128,16,4,256]{1,4,3,0,2:T(8,128)(2,1)} copy(bf16[2,128,16,4,256]{1,4,0,2,3:T(8,128)(2,1)} %bitcast.3) | data formatting | bytes 16777216 | tf_op jit(solution)/shard_map/reshape | solution.py:23
  242.0 0.0 copy-done.1
  242.0 11.6 %fusion.1 = bf16[2,16,256,1024]{2,3,0,1:T(8,128)(2,1)} fusion(bf16[2,128,16,1024,1]{1,3,0,4,2:T(8,128)(2,1)} %bitcast.33, bf16[1,2,128,16,256]{4,2,1,0,3:T(8,128)(2,1)S(1)} %maximum_bitcast_fusion, bf16[1,2,128,16,256]{4,2,1,0,3:T(8,128)(2,1)S(1)} %bitcast.36), kind=kOutput, calls=%fused_computation.2 | convolution fusion | flops 4320133120 | bytes 29360128 | tf_op jit(solution)/shard_map/ocsfa,csfb->ofab/dot_general | solution.py:10
  253.5 22.4 %copy.12 = bf16[2,16,256,1024]{3,2,1,0:T(8,128)(2,1)} copy(bf16[2,16,256,1024]{2,3,0,1:T(8,128)(2,1)} %fusion.1) | data formatting | bytes 33554432 | tf_op jit(solution)/shard_map/convert_element_type | solution.py:28
Async XLA Ops:
  34.4 1.4 copy-start
  45.5 188.4 %all-to-all-start.1 = ((bf16[4,2,128,16,256]{2,4,1,3,0:T(8,128)(2,1)}), bf16[4,2,128,16,256]{2,4,1,3,0:T(8,128)(2,1)}, u32[]{:S(2)}, u32[]{:S(2)}) async-start(bf16[4,2,128,16,256]{2,4,1,3,0:T(8,128)(2,1)} %stack.23), calls=%async_computation.1 | async-start | bytes 16777216 | tf_op jit(solution)/shard_map/all_to_all | solution.py:24
  233.9 8.0 %copy-start.1 = (bf16[2,8,16,16,256]{4,2,1,0,3:T(8,128)(2,1)S(1)}, bf16[2,8,16,16,256]{4,2,1,0,3:T(8,128)(2,1)}, u32[]{:S(2)}) copy-start(bf16[2,8,16,16,256]{4,2,1,0,3:T(8,128)(2,1)} %copy.11) | copy-start | bytes 6291460
